TPU v7x, 32 devices: a whole 2x2x4 slice. The times are simulated.
32 devices in a mesh: row: 4 (over z), col: 8 (over y, x, core).
Axes of the slice: x: 2, y: 2, z: 4, core: 2. Of those that a mesh axis runs over, the one named last changes fastest.
Arguments:
- hessian: float32 [16384, 4, 8, 512], P('row', None, 'col'), may hold values from -1 to 16, as said below
- weights: bfloat16 [512, 16384], P('col', 'row'), may hold values from -6 to 6
- codes: int32 [512, 8192], P('col', 'row'), may hold values from 0 to 255
- tile_map: int32 [32, 64], P('col', 'row'), may hold values from 0 to 511
- codebooks: float32 [512, 2, 256], replicated, may hold values from -6 to 6
Outputs:
- adjusted_codebooks: float32 [512, 2, 256], replicated
Inputs may be any that keep to these rules, and one draw needn't show every extreme that they name: `hessian`: H is symmetric with a dominant positive diagonal.
All inputs are finite; a program needn't handle non-finite values.
Results may differ from a plain program's by a relative error of at most 0.0003.
Values sent between devices are 32-bit elements; how exact they have to be, the bound alone decides.
A program may use at most 192 MiB of HBM per device.

v0:
```python
import jax
import jax.numpy as jnp
from jax import lax
from jax.sharding import PartitionSpec as P

CODES = 256
NB = 512
TILE_ROWS = 16
TILE_COLS = 256
STEPS = 2


learn_rate = 0.01


def per_device(hessian, weights, codes, tile_map, codebooks):
    rows_local, cols_local = weights.shape
    rows_tiles = rows_local // TILE_ROWS
    cols_tiles = cols_local // TILE_COLS
    tile_count = rows_tiles * cols_tiles
    half_width = TILE_COLS // 2
    pair_count = TILE_ROWS * half_width
    hessian_tile = hessian.reshape(
        hessian.shape[0], hessian.shape[1] * hessian.shape[2] * hessian.shape[3]
    )
    code_tiles = (
        codes.reshape(rows_tiles, TILE_ROWS, cols_tiles, half_width)
        .transpose(0, 2, 1, 3)
        .reshape(tile_count, pair_count)
    )
    code_onehot = (
        code_tiles[:, :, None] == lax.broadcasted_iota(jnp.int32, (1, 1, CODES), 2)
    ).astype(jnp.float32)
    book_onehot = (
        tile_map.reshape(-1)[:, None] == lax.broadcasted_iota(jnp.int32, (1, NB), 1)
    ).astype(jnp.float32)
    for iteration in range(STEPS):
        tile_books = jnp.einsum(
            "tb,bck->tck", book_onehot, codebooks, precision=lax.Precision.HIGHEST
        )
        rebuilt_tiles = jnp.einsum(
            "tpk,tck->tpc", code_onehot, tile_books, precision=lax.Precision.HIGHEST
        )
        rebuilt = (
            rebuilt_tiles.reshape(rows_tiles, cols_tiles, TILE_ROWS, half_width, 2)
            .transpose(0, 2, 1, 3, 4)
            .reshape(rows_local, cols_local)
        )
        error = rebuilt - weights.astype(jnp.float32)
        error_piece = lax.all_to_all(error, "col", split_axis=1, concat_axis=0, tiled=True)
        error_spread = lax.all_gather(error_piece, "row", axis=1, tiled=True)
        weight_grad = 2.0 * lax.psum_scatter(
            lax.dot_general(
                error_spread,
                hessian_tile,
                (((1,), (1,)), ((), ())),
                precision=lax.Precision.HIGHEST,
                preferred_element_type=jnp.float32,
            ),
            "col",
            scatter_dimension=0,
            tiled=True,
        )
        grad_tiles = (
            weight_grad.reshape(rows_tiles, TILE_ROWS, cols_tiles, half_width, 2)
            .transpose(0, 2, 1, 3, 4)
            .reshape(tile_count, pair_count, 2)
        )
        tile_grads = jnp.einsum(
            "tpk,tpc->tck", code_onehot, grad_tiles, precision=lax.Precision.HIGHEST
        )
        local_grad = jnp.einsum(
            "tb,tck->bck", book_onehot, tile_grads, precision=lax.Precision.HIGHEST
        )
        total_even, total_odd = lax.psum((local_grad[:, 0, :], local_grad[:, 1, :]), ("row", "col"))
        book_grad = jnp.stack([total_even, total_odd], axis=1)
        codebooks = codebooks - learn_rate * book_grad
    return codebooks


def solution(mesh):
    placed = (P("row", None, "col", None), P("col", "row"), P("col", "row"), P("col", "row"), P())
    return jax.shard_map(per_device, mesh=mesh, in_specs=placed, out_specs=P(), check_vma=False)
```

profile of v0, /device:TPU:1, one launch (start us, length us, event | category | flops | bytes accessed | tf_op | source)
XLA Modules:
  0.0 1100.1 jit_solution(13116930296548509444)
XLA Ops:
  6.5 0.8 eq.30
  7.3 1.1 copy.32
  8.8 2.0 fusion.10
  10.8 68.2 %fusion.3 = f32[64,2048,2]{1,2,0:T(2,128)S(1)} fusion(s32[64,2048]{1,0:T(8,128)S(1)} %bitcast.70, f32[64,2,256]{2,0,1:T(8,128)S(1)} %fusion.10), kind=kOutput, calls=%fused_computation.4 | convolution fusion | flops 838860800 | bytes 1703936 | tf_op jit(solution)/shard_map/tpk,tck->tpc/dot_general | solution.py:41
  79.0 0.8 reshape.39
  79.8 0.5 copy.12
  80.3 5.8 copy.11
  86.1 6.5 reshape.40
  92.6 1.5 convert_subtract_fusion.1
  94.2 2.2 copy.13
  96.3 19.2 %all_to_all.38 = f32[64,8,512]{2,0,1:T(8,128)} all-to-all(f32[64,8,512]{2,0,1:T(8,128)S(1)} %copy.13), channel_id=1, replica_groups=mesh['row'=4,'col'=8] {'col'}, dimensions={1} | all-to-all | bytes 2097152 | tf_op jit(solution)/shard_map/all_to_all | solution.py:50
  115.8 101.8 %reduce = f32[4096,4,512]{2,1,0:T(4,128)} reduce(f32[4096,4,1,512]{3,2,1,0:T(1,128)} %param.5, f32[]{:T(128)} %constant.6), dimensions={2}, to_apply=%param.5.reduce_sub_computation | reduce | bytes 67108864 | tf_op args[0]
  217.6 29.9 %copy.34 = f32[512,8,4,512]{3,1,2,0:T(8,128)} copy(f32[512,8,4,512]{3,2,1,0:T(4,128)} %bitcast.56) | data formatting | bytes 67108864
  247.5 59.3 %fusion.33 = f32[512,4096]{1,0:T(8,128)} fusion(f32[512,2048]{1,0:T(8,128)} %all-gather.3.cloned.1.call-done, f32[4096,2048]{1,0:T(8,128)} %bitcast.61), kind=kOutput, calls=%fused_computation.37 | convolution fusion | flops 51539607552 | bytes 46137344 | tf_op jit(solution)/shard_map/dot_general | solution.py:53
  306.9 71.4 %reduce-scatter.3.cloned.1.call-done = f32[64,4096]{1,0:T(8,128)} async-done(((f32[512,4096]{1,0:T(8,128)}), f32[64,4096]{1,0:T(8,128)}) %reduce-scatter.3.cloned.1.call-update) | async-done | bytes 1048592 | tf_op jit(solution)/shard_map/reduce_scatter | solution.py:52
  378.3 2.3 broadcast_multiply_fusion.1
  380.5 1.8 copy.14
  382.4 5.5 reshape.42
  387.9 6.7 copy.28
  394.5 0.6 reshape.53
  395.1 46.3 %fusion.2 = f32[64,2,256]{2,1,0:T(2,128)S(1)} fusion(f32[64,2048,2]{1,2,0:T(2,128)S(1)} %reshape.53, s32[64,2048]{1,0:T(8,128)} %bitcast.71), kind=kOutput, calls=%fused_computation.3 | convolution fusion | flops 838860800 | bytes 1703936 | tf_op jit(solution)/shard_map/tpk,tpc->tck/dot_general | solution.py:69
  441.4 0.7 fusion.17
  442.1 1.0 fusion.32
  443.1 0.3 all-gather.5.cloned.1.call-start
  443.4 130.3 %all-reduce.7.cloned.1.call-done = (f32[512,1,256]{2,0,1:T(8,128)}, f32[512,1,256]{2,0,1:T(8,128)}) async-done(((f32[512,1,256]{2,0,1:T(8,128)}, f32[512,1,256]{2,0,1:T(8,128)}), (f32[512,1,256]{2,0,1:T(8,128)}, f32[512,1,256]{2,0,1:T(8,128)})) %all-reduce.7.cloned.1.call-update) | async-done | bytes 1048592 | tf_op jit(solution)/shard_map/psum | solution.py:75
  573.7 1.8 fusion.12
  575.5 69.8 %fusion.1 = f32[64,2048,2]{1,2,0:T(2,128)} fusion(s32[64,2048]{1,0:T(8,128)} %bitcast.72, f32[64,2,256]{2,0,1:T(8,128)S(1)} %fusion.12), kind=kOutput, calls=%fused_computation.2 | convolution fusion | flops 838860800 | bytes 1703936 | tf_op jit(solution)/shard_map/tpk,tck->tpc/dot_general | solution.py:41
  645.2 2.1 reshape.44
  647.3 5.8 copy.17
  653.1 7.6 reshape.45
  660.7 3.1 convert_subtract_fusion
  663.8 2.2 copy.18
  666.0 19.2 %all_to_all.39 = f32[64,8,512]{2,0,1:T(8,128)} all-to-all(f32[64,8,512]{2,0,1:T(8,128)S(1)} %copy.18), channel_id=1, replica_groups=mesh['row'=4,'col'=8] {'col'}, dimensions={1} | all-to-all | bytes 2097152 | tf_op jit(solution)/shard_map/all_to_all | solution.py:50
  685.2 78.9 %all-gather.5.cloned.1.call-done = f32[512,2048]{1,0:T(8,128)} async-done(((f32[512,512]{1,0:T(8,128)}), f32[512,2048]{1,0:T(8,128)}) %all-gather.5.cloned.1.call-update) | async-done | bytes 4194320 | tf_op jit(solution)/shard_map/all_gather | solution.py:51
  764.2 59.3 %fusion.34 = f32[512,4096]{1,0:T(8,128)} fusion(f32[512,2048]{1,0:T(8,128)} %all-gather.5.cloned.1.call-done, f32[4096,2048]{1,0:T(8,128)} %bitcast.62), kind=kOutput, calls=%fused_computation.38 | convolution fusion | flops 51539607552 | bytes 46137344 | tf_op jit(solution)/shard_map/dot_general | solution.py:53
  823.5 0.3 all-reduce.5.cloned.1.call-start
  823.8 69.8 %reduce-scatter.5.cloned.1.call-done = f32[64,4096]{1,0:T(8,128)} async-done(((f32[512,4096]{1,0:T(8,128)}), f32[64,4096]{1,0:T(8,128)}) %reduce-scatter.5.cloned.1.call-update) | async-done | bytes 1048592 | tf_op jit(solution)/shard_map/reduce_scatter | solution.py:52
  893.6 1.3 broadcast_multiply_fusion
  894.9 2.0 copy.19
  896.9 7.3 reshape.46
  904.2 6.7 copy.29
  910.8 0.6 reshape.54
  911.4 46.3 %fusion = f32[64,2,256]{2,1,0:T(2,128)S(1)} fusion(f32[64,2048,2]{1,2,0:T(2,128)S(1)} %reshape.54, s32[64,2048]{1,0:T(8,128)} %bitcast.73), kind=kOutput, calls=%fused_computation.1 | convolution fusion | flops 838860800 | bytes 1703936 | tf_op jit(solution)/shard_map/tpk,tpc->tck/dot_general | solution.py:69
  957.7 0.7 fusion.14
  958.4 1.1 fusion.31
  959.5 130.6 %all-reduce.5.cloned.1.call-done = (f32[512,1,256]{2,0,1:T(8,128)}, f32[512,1,256]{2,0,1:T(8,128)}) async-done(((f32[512,1,256]{2,0,1:T(8,128)}, f32[512,1,256]{2,0,1:T(8,128)}), (f32[512,1,256]{2,0,1:T(8,128)}, f32[512,1,256]{2,0,1:T(8,128)})) %all-reduce.5.cloned.1.call-update) | async-done | bytes 1048592 | tf_op jit(solution)/shard_map/psum | solution.py:75
  1090.1 1.4 fusion.9
  1091.5 1.8 copy.21
  (23 shorter events, 0.8 us)
Async XLA Ops:
  6.5 241.0 %all-gather.3.cloned.1.call-start = ((), (), s32[]{:S(2)}) async-start(), calls=%async_computation.4 | async-start | bytes 5242880 | tf_op jit(solution)/shard_map/all_gather | solution.py:51
  8.8 2.0 copy-start.4
  10.8 69.1 %copy-start.3 = (bf16[64,4096]{1,0:T(8,128)(2,1)S(1)}, bf16[64,4096]{1,0:T(8,128)(2,1)}, u32[]{:S(2)}) copy-start(bf16[64,4096]{1,0:T(8,128)(2,1)} %param.6) | copy-start | bytes 1572868
  115.6 262.7 %reduce-scatter.3.cloned.1.call-start = ((), (), s32[]{:S(2)}) async-start(), calls=%async_computation.5 | async-start | bytes 9437184 | tf_op jit(solution)/shard_map/reduce_scatter | solution.py:52
  306.9 266.8 %all-reduce.7.cloned.1.call-start = ((), (), s32[]{:S(2)}) async-start(), calls=%async_computation.9 | async-start | bytes 2097152 | tf_op jit(solution)/shard_map/psum | solution.py:75
  395.1 178.6 %copy-start = (f32[512,2,256]{2,1,0:T(2,128)S(1)}, f32[512,2,256]{2,1,0:T(2,128)}, u32[]{:S(2)}) copy-start(f32[512,2,256]{2,1,0:T(2,128)} %param.9) | copy-start | bytes 3145732
  443.1 321.0 %all-gather.5.cloned.1.call-start = ((), (), s32[]{:S(2)}) async-start(), calls=%async_computation.6 | async-start | bytes 5242880 | tf_op jit(solution)/shard_map/all_gather | solution.py:51
  685.2 208.4 %reduce-scatter.5.cloned.1.call-start = ((), (), s32[]{:S(2)}) async-start(), calls=%async_computation.7 | async-start | bytes 9437184 | tf_op jit(solution)/shard_map/reduce_scatter | solution.py:52
  823.5 266.6 %all-reduce.5.cloned.1.call-start = ((), (), s32[]{:S(2)}) async-start(), calls=%async_computation.8 | async-start | bytes 2097152 | tf_op jit(solution)/shard_map/psum | solution.py:75
  911.4 178.7 %copy-start.1 = (f32[512,1,256]{2,0,1:T(8,128)S(1)}, f32[512,1,256]{2,0,1:T(8,128)}, u32[]{:S(2)}) copy-start(f32[512,1,256]{2,0,1:T(8,128)} %get-tuple-element.7) | copy-start | bytes 1572868
  911.4 178.7 %copy-start.2 = (f32[512,1,256]{2,0,1:T(8,128)S(1)}, f32[512,1,256]{2,0,1:T(8,128)}, u32[]{:S(2)}) copy-start(f32[512,1,256]{2,0,1:T(8,128)} %get-tuple-element.8) | copy-start | bytes 1572868
Sparse Core Ops, SparseCore 0:
  115.7 80.5 all-gather.2
  307.0 71.2 reduce-scatter.2
  443.3 130.3 all-reduce.6
  685.3 78.7 all-gather.4
  823.6 69.9 reduce-scatter.4
  959.6 130.4 all-reduce.4
where the time goes:
time: 1100 us
  waiting for transfers between devices  481 us (44%)
  matrix products  354 us (32%)
  other arithmetic  111 us (10%)
  local copies, waits for them, and re-layouts  100 us (9%)
  blocking collectives  38.4 us (3%)
  between operations  13.7 us (1%)
    psum x2, waiting for transfers between devices, per_device(): lax.psum((local_grad[:, 0, :], local_grad[:, 1, :]), ('row', 'col'))  261 us
    reduce_scatter x2, waiting for transfers between devices, per_device(): lax.psum_scatter(lax.dot_general(error_spread, hessian_tile, (((1,), (1,)...  141 us
    dot_general x2, matrix products, per_device(): jnp.einsum('tpk,tck->tpc', code_onehot, tile_books, precision=lax.Precisi...  138 us
    dot_general x2, matrix products, per_device(): lax.dot_general(error_spread, hessian_tile, (((1,), (1,)), ((), ())), pre...  119 us
    unnamed x1, other arithmetic  102 us
    dot_general x2, matrix products, per_device(): jnp.einsum('tpk,tpc->tck', code_onehot, grad_tiles, precision=lax.Precisi...  92.5 us
    all_gather x2, waiting for transfers between devices, per_device(): error_spread = lax.all_gather(error_piece, 'row', axis=1, tiled=True)  78.9 us
    all_to_all x2, blocking collectives, per_device(): lax.all_to_all(error, 'col', split_axis=1, concat_axis=0, tiled=True)  38.4 us
  transfers between devices with their start and end apart: 6, of which 5 were waited for; matrix products, arithmetic and copies ran while one was open for 12% of the time, Pallas kernels for 0%

commit v1 on v0

v1 whole, which is shorter than its diff:
```python
import functools

import jax
import jax.numpy as jnp
from jax import lax
from jax.experimental import pallas as pl
from jax.experimental.pallas import tpu as pltpu
from jax.sharding import PartitionSpec as P

TILE_ROWS = 16
TILE_COLS = 256
STEPS = 2
LANES = 128
HALF = TILE_COLS // 2

learn_rate = 0.01
MESH = pl.DeviceIdType.MESH
NT = (((1,), (1,)), ((), ()))


def split_kernel(hessian_ref, high_ref, low_ref):
    rows, width = high_ref.shape
    stride = width // LANES
    for k in range(stride):
        x = hessian_ref[pl.ds(k, rows, stride=stride), :]
        high = x.astype(jnp.bfloat16)
        high_ref[:, k * LANES : (k + 1) * LANES] = high
        low_ref[:, k * LANES : (k + 1) * LANES] = (x - high.astype(jnp.float32)).astype(jnp.bfloat16)


def split_hessian(hessian):
    rows = hessian.shape[0]
    width = hessian.shape[1] * hessian.shape[2] * hessian.shape[3]
    stride = width // LANES
    block = min(rows, 256)
    part = jax.ShapeDtypeStruct((rows, width), jnp.bfloat16)
    spec = pl.BlockSpec((block, width), lambda i: (i, 0))
    return pl.pallas_call(
        split_kernel,
        grid=(rows // block,),
        in_specs=[pl.BlockSpec((block * stride, LANES), lambda i: (i, 0))],
        out_specs=[spec, spec],
        out_shape=[part, part],
        cost_estimate=pl.CostEstimate(flops=rows * width * 4, bytes_accessed=rows * width * 8, transcendentals=0),
        name="split_hessian",
    )(hessian.reshape(rows * stride, LANES))


def pick(table, index):
    return jnp.take_along_axis(table, index, axis=1, mode="promise_in_bounds")


def error_kernel(map_ref, codes_ref, weights_ref, books_ref, error_ref):
    tiles_down, tiles_across = map_ref.shape
    shape = (TILE_ROWS, LANES)
    lane = lax.broadcasted_iota(jnp.int32, shape, 1)
    odd = (lane & 1) == 1

    def tile(t, carry):
        i, j = t // tiles_across, t % tiles_across
        table = books_ref[map_ref[i, j]]
        rows = pl.ds(pl.multiple_of(i * TILE_ROWS, TILE_ROWS), TILE_ROWS)
        codes = codes_ref[rows, pl.ds(pl.multiple_of(j * HALF, HALF), HALF)]
        tables = [jnp.broadcast_to(table[n : n + 1, :], shape) for n in range(4)]
        for half in range(2):
            code = pick(codes, (lane >> 1) + half * (LANES // 2))
            index = code & (LANES - 1)
            upper = code >= LANES
            near = jnp.where(odd, pick(tables[1], index), pick(tables[0], index))
            far = jnp.where(odd, pick(tables[3], index), pick(tables[2], index))
            columns = pl.ds(pl.multiple_of(j * TILE_COLS + half * LANES, LANES), LANES)
            error_ref[rows, columns] = jnp.where(upper, far, near) - weights_ref[rows, columns].astype(jnp.float32)
        return carry

    lax.fori_loop(0, tiles_down * tiles_across, tile, 0, unroll=2)


VMEM = pl.BlockSpec(memory_space=pltpu.VMEM)
SMEM = pl.BlockSpec(memory_space=pltpu.SMEM)


def errors(tile_map, codes, weights, books):
    return pl.pallas_call(
        error_kernel,
        in_specs=[SMEM, VMEM, VMEM, VMEM],
        out_specs=VMEM,
        out_shape=jax.ShapeDtypeStruct(weights.shape, jnp.float32),
        name="errors",
    )(tile_map, codes, weights, books.reshape(-1, 4, LANES))


def product_kernel(error_ref, high_ref, low_ref, out_ref, error_high, error_low):
    @pl.when(pl.program_id(0) == 0)
    def _():
        x = error_ref[...]
        high = x.astype(jnp.bfloat16)
        error_high[...] = high
        error_low[...] = (x - high.astype(jnp.float32)).astype(jnp.bfloat16)

    dot = functools.partial(lax.dot_general, dimension_numbers=NT, preferred_element_type=jnp.float32)
    total = dot(error_high[...], low_ref[...]) + dot(error_low[...], high_ref[...])
    out_ref[...] = total + dot(error_high[...], high_ref[...])


def product(error, high, low):
    m, k = error.shape
    n = high.shape[0]
    block = min(n, 512)
    spec = pl.BlockSpec((block, k), lambda i: (i, 0))
    return pl.pallas_call(
        product_kernel,
        grid=(n // block,),
        in_specs=[pl.BlockSpec((m, k), lambda i: (0, 0)), spec, spec],
        out_specs=pl.BlockSpec((m, block), lambda i: (0, i)),
        out_shape=jax.ShapeDtypeStruct((m, n), jnp.float32),
        scratch_shapes=[pltpu.VMEM((m, k), jnp.bfloat16), pltpu.VMEM((m, k), jnp.bfloat16)],
        cost_estimate=pl.CostEstimate(flops=6 * m * n * k, bytes_accessed=4 * n * k + 4 * m * (n + k), transcendentals=0),
        name="product",
    )(error, high, low)


def scatter_kernel(map_ref, codes_ref, grad_ref, books_ref):
    tiles_down, tiles_across = map_ref.shape
    shape = (TILE_ROWS, LANES)
    lane = lax.broadcasted_iota(jnp.int32, shape, 1)
    first = lane < LANES // 2
    even_index = (2 * lane) & (LANES - 1)
    line = lax.broadcasted_iota(jnp.int32, (8, LANES), 0)
    is_odd = (line & 1) == 1
    is_upper = (line & 2) == 2
    is_low = lax.broadcasted_iota(jnp.int32, (8, HALF * TILE_ROWS), 0) >= 4
    entry = lax.broadcasted_iota(jnp.int32, (LANES, LANES), 0)
    books_ref[...] = jnp.zeros_like(books_ref)

    def tile(t, carry):
        i, j = t // tiles_across, t % tiles_across
        rows = pl.ds(pl.multiple_of(i * TILE_ROWS, TILE_ROWS), TILE_ROWS)
        codes = codes_ref[rows, pl.ds(pl.multiple_of(j * HALF, HALF), HALF)]
        left = grad_ref[rows, pl.ds(pl.multiple_of(j * TILE_COLS, LANES), LANES)]
        right = grad_ref[rows, pl.ds(pl.multiple_of(j * TILE_COLS + LANES, LANES), LANES)]
        even = jnp.where(first, pick(left, even_index), pick(right, even_index))
        odd = jnp.where(first, pick(left, even_index + 1), pick(right, even_index + 1))
        index = codes & (LANES - 1)
        upper = jnp.where(codes >= LANES, 1, 0)
        values, hots = [], []
        for n in range(TILE_ROWS):
            value = jnp.where(is_odd, odd[n : n + 1, :], even[n : n + 1, :])
            fits = is_upper == (jnp.broadcast_to(upper[n : n + 1, :], (8, LANES)) == 1)
            values.append(jnp.where(fits, value, 0.0))
            hots.append(jnp.where(entry == index[n : n + 1, :], 1.0, 0.0).astype(jnp.bfloat16))
        value = jnp.concatenate(values, axis=1)
        high = value.astype(jnp.bfloat16).astype(jnp.float32)
        parts = jnp.where(is_low, value - high, high).astype(jnp.bfloat16)
        sums = lax.dot_general(parts, jnp.concatenate(hots, axis=1), NT, preferred_element_type=jnp.float32)
        book = map_ref[i, j]
        books_ref[book] += sums[0:4, :] + sums[4:8, :]
        return carry

    lax.fori_loop(0, tiles_down * tiles_across, tile, 0)


def scatter(tile_map, codes, grad, books):
    total = pl.pallas_call(
        scatter_kernel,
        in_specs=[SMEM, VMEM, VMEM],
        out_specs=VMEM,
        out_shape=jax.ShapeDtypeStruct((books.shape[0] // 4, 4, LANES), jnp.float32),
        name="scatter",
    )(tile_map, codes, grad)
    return total.reshape(books.shape)


def update_kernel(n_row, n_col, grad_ref, books_ref, out_ref, col_in, row_sum, row_in, col_send, col_recv, row_send, row_recv, row_send2, row_recv2, col_send2, col_recv2):
    r, c = lax.axis_index("row"), lax.axis_index("col")
    wide = grad_ref.shape[0] // n_col
    thin = wide // n_row
    cols = [lax.rem(c + d, n_col) for d in range(n_col)]
    rows = [lax.rem(r + d, n_row) for d in range(n_row)]

    barrier = pltpu.get_barrier_semaphore()
    for d in range(1, n_col):
        pl.semaphore_signal(barrier, inc=1, device_id=(r, cols[d]), device_id_type=MESH)
    for d in range(1, n_row):
        pl.semaphore_signal(barrier, inc=1, device_id=(rows[d], c), device_id_type=MESH)
    pl.semaphore_wait(barrier, n_col + n_row - 2)

    def piece(index, size):
        return pl.ds(pl.multiple_of(index * size, size), size)

    def send(src, dst, sends, recvs, d, device):
        copy = pltpu.make_async_remote_copy(
            src_ref=src, dst_ref=dst, send_sem=sends.at[d], recv_sem=recvs.at[d], device_id=device, device_id_type=MESH
        )
        copy.start()
        return copy

    first = [
        send(grad_ref.at[piece(cols[d], wide)], col_in.at[d], col_send, col_recv, d, (r, cols[d])) for d in range(1, n_col)
    ]
    total = grad_ref[piece(c, wide), :]
    for d, copy in enumerate(first, 1):
        copy.wait_recv()
        total = total + col_in[d]
    row_sum[...] = total
    second = [
        send(row_sum.at[piece(rows[d], thin)], row_in.at[d], row_send, row_recv, d, (rows[d], c)) for d in range(1, n_row)
    ]
    total = row_sum[piece(r, thin), :]
    for d, copy in enumerate(second, 1):
        copy.wait_recv()
        total = total + row_in[d]
    mine = piece(c * n_row + r, thin)
    out_ref[mine, :] = books_ref[mine, :] - learn_rate * (2.0 * total)
    third = [send(out_ref.at[mine], out_ref.at[mine], row_send2, row_recv2, d, (rows[d], c)) for d in range(1, n_row)]
    for copy in third:
        copy.wait_recv()
    whole = piece(c, wide)
    fourth = [send(out_ref.at[whole], out_ref.at[whole], col_send2, col_recv2, d, (r, cols[d])) for d in range(1, n_col)]
    for copy in fourth:
        copy.wait_recv()
    for copy in first + second + third + fourth:
        copy.wait_send()


def update(n_row, n_col, grad, books):
    wide = books.shape[0] // n_col
    thin = wide // n_row
    dma = pltpu.SemaphoreType.DMA
    return pl.pallas_call(
        functools.partial(update_kernel, n_row, n_col),
        in_specs=[VMEM, VMEM],
        out_specs=VMEM,
        out_shape=jax.ShapeDtypeStruct(books.shape, jnp.float32),
        scratch_shapes=[
            pltpu.VMEM((n_col, wide, LANES), jnp.float32),
            pltpu.VMEM((wide, LANES), jnp.float32),
            pltpu.VMEM((n_row, thin, LANES), jnp.float32),
            dma((n_col,)),
            dma((n_col,)),
            dma((n_row,)),
            dma((n_row,)),
            dma((n_row,)),
            dma((n_row,)),
            dma((n_col,)),
            dma((n_col,)),
        ],
        compiler_params=pltpu.CompilerParams(collective_id=0, has_side_effects=True),
        name="update",
    )(grad, books)


def per_device(n_row, n_col, hessian, weights, codes, tile_map, codebooks):
    count, parts, entries = codebooks.shape
    books = codebooks.reshape(count, parts, entries // LANES, LANES).transpose(0, 2, 1, 3).reshape(-1, LANES)
    high, low = split_hessian(hessian)
    for step in range(STEPS):
        error = errors(tile_map, codes, weights, books)
        piece = lax.all_to_all(error, "col", split_axis=1, concat_axis=0, tiled=True)
        spread = lax.all_gather(piece, "row", axis=1, tiled=True)
        partial = product(spread, high, low)
        grad = lax.psum_scatter(partial, "col", scatter_dimension=0, tiled=True)
        books = update(n_row, n_col, scatter(tile_map, codes, grad, books), books)
    return books.reshape(count, entries // LANES, parts, LANES).transpose(0, 2, 1, 3).reshape(codebooks.shape)


def solution(mesh):
    placed = (P("row", None, "col", None), P("col", "row"), P("col", "row"), P("col", "row"), P())
    body = functools.partial(per_device, mesh.shape["row"], mesh.shape["col"])
    return jax.shard_map(body, mesh=mesh, in_specs=placed, out_specs=P(), check_vma=False)
```

time: 1100 us -> 566 us (0.51)
  matrix products: 354 us -> 0 us
  Pallas kernels: 0 us -> 244 us
  waiting for transfers between devices: 481 us -> 266 us
  other arithmetic: 111 us -> 0 us
  local copies, waits for them, and re-layouts: 100 us -> 5.17 us
    dot_general x10 -> x0, matrix products: 354 us -> none  [the longest x2 138 us: per_device(): jnp.einsum('tpk,tck->tpc', code_onehot, tile_books, precision=lax.Precisi...]
    psum x2 -> x0, waiting for transfers between devices: 261 us -> none  [per_device(): lax.psum((local_grad[:, 0, :], local_grad[:, 1, :]), ('row', 'col'))]
    pallas_call x0 -> x9, Pallas kernels: none -> 244 us  [the longest x2 80.4 us: update(): pl.pallas_call(functools.partial(update_kernel, n_row, n_col), in_specs=[...]
    unnamed x1 -> x0, other arithmetic: 102 us -> none
    reshape x13 -> x0, local copies, waits for them, and re-layouts: 56 us -> none  [the longest x4 14.5 us: per_device(): rebuilt_tiles.reshape(rows_tiles, cols_tiles, TILE_ROWS, half_width, 2)]
    all_gather x2, waiting for transfers between devices: 78.9 us -> 126 us  [per_device(): spread = lax.all_gather(piece, 'row', axis=1, tiled=True)]
    unnamed x14 -> x1, local copies, waits for them, and re-layouts: 31.7 us -> 2.55 us
  transfers between devices with their start and end apart: 6 -> 4, of which waited for: 5 -> 4; matrix products, arithmetic and copies ran while one was open for 12% -> 0% of each run, Pallas kernels for 0% -> 6%
where the time goes in v1:
time: 566 us; the launch traced here: 565 us
  waiting for transfers between devices  266 us (47%)
  Pallas kernels  244 us (43%)
  blocking collectives  36.1 us (6%)
  between operations  13.2 us (2%)
    reduce_scatter x2, waiting for transfers between devices, per_device(): grad = lax.psum_scatter(partial, 'col', scatter_dimension=0, tiled=True)  140 us
    all_gather x2, waiting for transfers between devices, per_device(): spread = lax.all_gather(piece, 'row', axis=1, tiled=True)  126 us
    pallas_call x2, Pallas kernels, update(): pl.pallas_call(functools.partial(update_kernel, n_row, n_col), in_specs=[...  80.4 us
    pallas_call x2, Pallas kernels, product(): pl.pallas_call(product_kernel, grid=(n // block,), in_specs=[pl.BlockSpec...  65.7 us
    pallas_call x2, Pallas kernels, scatter(): pl.pallas_call(scatter_kernel, in_specs=[SMEM, VMEM, VMEM], out_specs=VME...  45 us
    all_to_all x2, blocking collectives, per_device(): lax.all_to_all(error, 'col', split_axis=1, concat_axis=0, tiled=True)  36.1 us
    pallas_call x1, Pallas kernels, split_hessian(): pl.pallas_call(split_kernel, grid=(rows // block,), in_specs=[pl.BlockSpe...  33.8 us
    pallas_call x2, Pallas kernels, errors(): pl.pallas_call(error_kernel, in_specs=[SMEM, VMEM, VMEM, VMEM], out_specs...  19.1 us
  transfers between devices with their start and end apart: 4, of which 4 were waited for; matrix products, arithmetic and copies ran while one was open for 0% of the time, Pallas kernels for 6%

profile of v1, /device:TPU:1, one launch (start us, length us, event | category | flops | bytes accessed | tf_op | source)
XLA Modules:
  0.0 564.8 jit_solution(8243831160894797628)
XLA Ops:
  6.5 0.0 all-gather.3.cloned.1.call-start
  6.5 9.6 %errors.2 = f32[64,4096]{1,0:T(8,128)} custom-call(s32[4,16]{1,0:T(4,128)} %map_ref.7, s32[64,2048]{1,0:T(8,128)} %codes_ref.7, bf16[64,4096]{1,0:T(8,128)(2,1)} %weights_ref.3, f32[512,4,128]{2,1,0:T(4,128)} %bitcast.35), custom_call_target="tpu_custom_call" | custom-call | tf_op jit(solution)/shard_map/errors/pallas_call | solution.py:83
  16.1 1.3 copy.15
  17.4 19.2 %all_to_all.38 = f32[64,8,512]{2,0,1:T(8,128)} all-to-all(f32[64,8,512]{2,0,1:T(8,128)S(1)} %bitcast.39), channel_id=1, replica_groups=mesh['row'=4,'col'=8] {'col'}, dimensions={1} | all-to-all | bytes 2097152 | tf_op jit(solution)/shard_map/all_to_all | solution.py:258
  36.6 0.0 all-gather.3.cloned.1.call-update
  36.7 0.0 reduce-scatter.3.cloned.1.call-start
  36.7 33.8 %split_hessian.1 = (bf16[4096,2048]{1,0:T(8,128)(2,1)}, bf16[4096,2048]{1,0:T(8,128)(2,1)}) custom-call(f32[65536,128]{1,0:T(8,128)} %bitcast.30), custom_call_target="tpu_custom_call" | custom-call | flops 33554432 | bytes 67108864 | tf_op jit(solution)/shard_map/split_hessian/pallas_call | solution.py:38
  70.5 46.9 %all-gather.3.cloned.1.call-done.error_ref = f32[512,2048]{1,0:T(8,128)} async-done(((f32[512,512]{1,0:T(8,128)}), f32[512,2048]{1,0:T(8,128)}) %all-gather.3.cloned.1.call-update) | async-done | bytes 4194320 | tf_op jit(solution)/shard_map/all_gather | solution.py:259
  117.3 32.8 %product.2 = f32[512,4096]{1,0:T(8,128)} custom-call(f32[512,2048]{1,0:T(8,128)} %all-gather.3.cloned.1.call-done.error_ref, bf16[4096,2048]{1,0:T(8,128)(2,1)} %get-tuple-element.7.high_ref, bf16[4096,2048]{1,0:T(8,128)(2,1)} %get-tuple-element.8.low_ref), custom_call_target="tpu_custom_call" | custom-call | flops 25769803776 | bytes 46137344 | tf_op jit(solution)/shard_map/product/pallas_call | solution.py:110
  150.2 0.0 reduce-scatter.3.cloned.1.call-update
  150.2 0.0 all-gather.5.cloned.1.call-start
  150.2 70.1 %reduce-scatter.3.cloned.1.call-done.grad_ref = f32[64,4096]{1,0:T(8,128)} async-done(((f32[512,4096]{1,0:T(8,128)}), f32[64,4096]{1,0:T(8,128)}) %reduce-scatter.3.cloned.1.call-update) | async-done | bytes 1048592 | tf_op jit(solution)/shard_map/reduce_scatter | solution.py:261
  220.3 22.5 %scatter.2 = f32[512,4,128]{2,1,0:T(4,128)} custom-call(s32[4,16]{1,0:T(4,128)} %map_ref.7, s32[64,2048]{1,0:T(8,128)} %codes_ref.7, f32[64,4096]{1,0:T(8,128)} %reduce-scatter.3.cloned.1.call-done.grad_ref), custom_call_target="tpu_custom_call" | custom-call | tf_op jit(solution)/shard_map/scatter/pallas_call | solution.py:163
  242.8 40.2 %update.2.books_ref = f32[2048,128]{1,0:T(8,128)} custom-call(f32[2048,128]{1,0:T(8,128)} %bitcast.34, f32[2048,128]{1,0:T(8,128)} %bitcast.36), custom_call_target="tpu_custom_call" | custom-call | tf_op jit(solution)/shard_map/update/pallas_call | solution.py:229
  283.0 9.6 %errors.3 = f32[64,4096]{1,0:T(8,128)} custom-call(s32[4,16]{1,0:T(4,128)} %map_ref.7, s32[64,2048]{1,0:T(8,128)} %codes_ref.7, bf16[64,4096]{1,0:T(8,128)(2,1)} %weights_ref.3, f32[512,4,128]{2,1,0:T(4,128)} %bitcast.31), custom_call_target="tpu_custom_call" | custom-call | tf_op jit(solution)/shard_map/errors/pallas_call | solution.py:83
  292.6 1.3 copy.14
  293.9 16.9 %all_to_all.39 = f32[64,8,512]{2,0,1:T(8,128)} all-to-all(f32[64,8,512]{2,0,1:T(8,128)S(1)} %bitcast.40), channel_id=1, replica_groups=mesh['row'=4,'col'=8] {'col'}, dimensions={1} | all-to-all | bytes 2097152 | tf_op jit(solution)/shard_map/all_to_all | solution.py:258
  310.8 0.0 all-gather.5.cloned.1.call-update
  310.8 0.0 reduce-scatter.5.cloned.1.call-start
  310.9 79.2 %all-gather.5.cloned.1.call-done.error_ref = f32[512,2048]{1,0:T(8,128)} async-done(((f32[512,512]{1,0:T(8,128)}), f32[512,2048]{1,0:T(8,128)}) %all-gather.5.cloned.1.call-update) | async-done | bytes 4194320 | tf_op jit(solution)/shard_map/all_gather | solution.py:259
  390.0 32.8 %product.3 = f32[512,4096]{1,0:T(8,128)} custom-call(f32[512,2048]{1,0:T(8,128)} %all-gather.5.cloned.1.call-done.error_ref, bf16[4096,2048]{1,0:T(8,128)(2,1)} %get-tuple-element.7.high_ref, bf16[4096,2048]{1,0:T(8,128)(2,1)} %get-tuple-element.8.low_ref), custom_call_target="tpu_custom_call" | custom-call | flops 25769803776 | bytes 46137344 | tf_op jit(solution)/shard_map/product/pallas_call | solution.py:110
  422.9 0.0 reduce-scatter.5.cloned.1.call-update
  422.9 70.1 %reduce-scatter.5.cloned.1.call-done.grad_ref = f32[64,4096]{1,0:T(8,128)} async-done(((f32[512,4096]{1,0:T(8,128)}), f32[64,4096]{1,0:T(8,128)}) %reduce-scatter.5.cloned.1.call-update) | async-done | bytes 1048592 | tf_op jit(solution)/shard_map/reduce_scatter | solution.py:261
  493.0 22.5 %scatter.3 = f32[512,4,128]{2,1,0:T(4,128)} custom-call(s32[4,16]{1,0:T(4,128)} %map_ref.7, s32[64,2048]{1,0:T(8,128)} %codes_ref.7, f32[64,4096]{1,0:T(8,128)} %reduce-scatter.5.cloned.1.call-done.grad_ref), custom_call_target="tpu_custom_call" | custom-call | tf_op jit(solution)/shard_map/scatter/pallas_call | solution.py:163
  515.5 40.2 %update.3 = f32[2048,128]{1,0:T(8,128)} custom-call(f32[2048,128]{1,0:T(8,128)} %bitcast.32, f32[2048,128]{1,0:T(8,128)} %update.2.books_ref), custom_call_target="tpu_custom_call" | custom-call | tf_op jit(solution)/shard_map/update/pallas_call | solution.py:229
  555.7 2.6 copy.17
Async XLA Ops:
  6.5 110.8 %all-gather.3.cloned.1.call-start = ((), (), s32[]{:S(2)}) async-start(), calls=%async_computation.4 | async-start | bytes 5242880 | tf_op jit(solution)/shard_map/all_gather | solution.py:259
  36.7 183.7 %reduce-scatter.3.cloned.1.call-start = ((), (), s32[]{:S(2)}) async-start(), calls=%async_computation.5 | async-start | bytes 9437184 | tf_op jit(solution)/shard_map/reduce_scatter | solution.py:261
  150.2 239.8 %all-gather.5.cloned.1.call-start = ((), (), s32[]{:S(2)}) async-start(), calls=%async_computation.6 | async-start | bytes 5242880 | tf_op jit(solution)/shard_map/all_gather | solution.py:259
  310.8 182.2 %reduce-scatter.5.cloned.1.call-start = ((), (), s32[]{:S(2)}) async-start(), calls=%async_computation.7 | async-start | bytes 9437184 | tf_op jit(solution)/shard_map/reduce_scatter | solution.py:261
Sparse Core Ops, SparseCore 0:
  36.8 80.5 all-gather.2
  150.3 69.9 reduce-scatter.2
  310.9 79.0 all-gather.4
  423.0 69.9 reduce-scatter.4

commit v2 on v1

--- a/solution.py
+++ b/solution.py
@@ -89,31 +89,108 @@
     )(tile_map, codes, weights, books.reshape(-1, 4, LANES))
 
 
-def product_kernel(error_ref, high_ref, low_ref, out_ref, error_high, error_low):
-    @pl.when(pl.program_id(0) == 0)
+def product_kernel(chunks, error_ref, high_ref, low_ref, out_ref, error_high, error_low, made, pair_in, pair_sum, chip_in, pair_send, pair_recv, chip_send, chip_recv):
+    n = pl.program_id(0)
+    r, c = lax.axis_index("row"), lax.axis_index("col")
+    chips = made.shape[1]
+    block = made.shape[4]
+    chip, core = c // 2, lax.rem(c, 2)
+    others = [lax.rem(chip + d, chips) for d in range(chips)]
+
+    @pl.when(n == 0)
     def _():
+        barrier = pltpu.get_barrier_semaphore()
+        pl.semaphore_signal(barrier, inc=1, device_id=(r, chip * 2 + 1 - core), device_id_type=MESH)
+        for d in range(1, chips):
+            pl.semaphore_signal(barrier, inc=1, device_id=(r, others[d] * 2 + core), device_id_type=MESH)
         x = error_ref[...]
         high = x.astype(jnp.bfloat16)
         error_high[...] = high
         error_low[...] = (x - high.astype(jnp.float32)).astype(jnp.bfloat16)
+        pl.semaphore_wait(barrier, chips)
+
+    def to_pair(k):
+        return pltpu.make_async_remote_copy(
+            src_ref=made.at[k, :, 1 - core],
+            dst_ref=pair_in.at[k],
+            send_sem=pair_send.at[k],
+            recv_sem=pair_recv.at[k],
+            device_id=(r, chip * 2 + 1 - core),
+            device_id_type=MESH,
+        )
+
+    def to_chip(k, d):
+        return pltpu.make_async_remote_copy(
+            src_ref=pair_sum.at[k, others[d]],
+            dst_ref=chip_in.at[d - 1, k],
+            send_sem=chip_send.at[d - 1, k],
+            recv_sem=chip_recv.at[d - 1, k],
+            device_id=(r, others[d] * 2 + core),
+            device_id_type=MESH,
+        )
+
+    def add_pair(k):
+        to_pair(k).wait_recv()
+        pair_sum[k] = made[k, :, core] + pair_in[k]
+        for d in range(1, chips):
+            to_chip(k, d).start()
 
     dot = functools.partial(lax.dot_general, dimension_numbers=NT, preferred_element_type=jnp.float32)
     total = dot(error_high[...], low_ref[...]) + dot(error_low[...], high_ref[...])
-    out_ref[...] = total + dot(error_high[...], high_ref[...])
-
-
-def product(error, high, low):
+    total = total + dot(error_high[...], high_ref[...])
+    made[n] = total.reshape(made.shape[1:])
+    to_pair(n).start()
+
+    @pl.when(n > 0)
+    def _():
+        add_pair(n - 1)
+
+    @pl.when(n == chunks - 1)
+    def _():
+        add_pair(n)
+
+        def finish(k, carry):
+            total = pair_sum[k, chip]
+            for d in range(1, chips):
+                to_chip(k, d).wait_recv()
+                total = total + chip_in[d - 1, k]
+            out_ref[:, pl.ds(pl.multiple_of(k * block, block), block)] = total
+            to_pair(k).wait_send()
+            for d in range(1, chips):
+                to_chip(k, d).wait_send()
+            return carry
+
+        lax.fori_loop(0, chunks, finish, 0)
+
+
+def product(n_col, error, high, low):
     m, k = error.shape
     n = high.shape[0]
     block = min(n, 512)
+    chunks = n // block
+    chips = n_col // 2
+    rows = m // n_col
     spec = pl.BlockSpec((block, k), lambda i: (i, 0))
+    dma = pltpu.SemaphoreType.DMA
     return pl.pallas_call(
-        product_kernel,
-        grid=(n // block,),
+        functools.partial(product_kernel, chunks),
+        grid=(chunks,),
         in_specs=[pl.BlockSpec((m, k), lambda i: (0, 0)), spec, spec],
-        out_specs=pl.BlockSpec((m, block), lambda i: (0, i)),
-        out_shape=jax.ShapeDtypeStruct((m, n), jnp.float32),
-        scratch_shapes=[pltpu.VMEM((m, k), jnp.bfloat16), pltpu.VMEM((m, k), jnp.bfloat16)],
+        out_specs=pl.BlockSpec((rows, n), lambda i: (0, 0)),
+        out_shape=jax.ShapeDtypeStruct((rows, n), jnp.float32),
+        scratch_shapes=[
+            pltpu.VMEM((m, k), jnp.bfloat16),
+            pltpu.VMEM((m, k), jnp.bfloat16),
+            pltpu.VMEM((chunks, chips, 2, rows, block), jnp.float32),
+            pltpu.VMEM((chunks, chips, rows, block), jnp.float32),
+            pltpu.VMEM((chunks, chips, rows, block), jnp.float32),
+            pltpu.VMEM((chips - 1, chunks, rows, block), jnp.float32),
+            dma((chunks,)),
+            dma((chunks,)),
+            dma((chips - 1, chunks)),
+            dma((chips - 1, chunks)),
+        ],
+        compiler_params=pltpu.CompilerParams(collective_id=1, has_side_effects=True, vmem_limit_bytes=56 * 2**20),
         cost_estimate=pl.CostEstimate(flops=6 * m * n * k, bytes_accessed=4 * n * k + 4 * m * (n + k), transcendentals=0),
         name="product",
     )(error, high, low)
@@ -257,8 +334,7 @@
         error = errors(tile_map, codes, weights, books)
         piece = lax.all_to_all(error, "col", split_axis=1, concat_axis=0, tiled=True)
         spread = lax.all_gather(piece, "row", axis=1, tiled=True)
-        partial = product(spread, high, low)
-        grad = lax.psum_scatter(partial, "col", scatter_dimension=0, tiled=True)
+        grad = product(n_col, spread, high, low)
         books = update(n_row, n_col, scatter(tile_map, codes, grad, books), books)
     return books.reshape(count, entries // LANES, parts, LANES).transpose(0, 2, 1, 3).reshape(codebooks.shape)
 

time: 566 us -> 478 us (0.84)
  waiting for transfers between devices: 266 us -> 127 us
  Pallas kernels: 244 us -> 295 us
    reduce_scatter x2 -> x0, waiting for transfers between devices: 140 us -> none  [per_device(): grad = lax.psum_scatter(partial, 'col', scatter_dimension=0, tiled=True)]
    pallas_call x2, Pallas kernels: 65.7 us -> 120 us  [product(): pl.pallas_call(functools.partial(product_kernel, chunks), grid=(chunks,),...]
  transfers between devices with their start and end apart: 4 -> 2, of which waited for: 4 -> 2; matrix products, arithmetic and copies ran while one was open for 0% -> 0% of each run, Pallas kernels for 6% -> 7%
where the time goes in v2:
time: 478 us; the launch traced here: 477 us
  Pallas kernels  295 us (62%)
  waiting for transfers between devices  127 us (27%)
  blocking collectives  36.1 us (8%)
  between operations  13.5 us (3%)
  local copies, waits for them, and re-layouts  5.17 us (1%)
    all_gather x2, waiting for transfers between devices, per_device(): spread = lax.all_gather(piece, 'row', axis=1, tiled=True)  127 us
    pallas_call x2, Pallas kernels, product(): pl.pallas_call(functools.partial(product_kernel, chunks), grid=(chunks,),...  120 us
    pallas_call x2, Pallas kernels, update(): pl.pallas_call(functools.partial(update_kernel, n_row, n_col), in_specs=[...  77.7 us
    pallas_call x2, Pallas kernels, scatter(): pl.pallas_call(scatter_kernel, in_specs=[SMEM, VMEM, VMEM], out_specs=VME...  45 us
    all_to_all x2, blocking collectives, per_device(): lax.all_to_all(error, 'col', split_axis=1, concat_axis=0, tiled=True)  36.1 us
    pallas_call x1, Pallas kernels, split_hessian(): pl.pallas_call(split_kernel, grid=(rows // block,), in_specs=[pl.BlockSpe...  33.8 us
    pallas_call x2, Pallas kernels, errors(): pl.pallas_call(error_kernel, in_specs=[SMEM, VMEM, VMEM, VMEM], out_specs...  19.1 us
  transfers between devices with their start and end apart: 2, of which 2 were waited for; matrix products, arithmetic and copies ran while one was open for 0% of the time, Pallas kernels for 7%

profile of v2, /device:TPU:1, one launch (start us, length us, event | category | flops | bytes accessed | tf_op | source)
XLA Modules:
  0.0 476.9 jit_solution(1767976405953112373)
XLA Ops:
  6.5 0.0 all-gather.3.cloned.1.call-start
  6.5 9.6 %errors.2 = f32[64,4096]{1,0:T(8,128)} custom-call(s32[4,16]{1,0:T(4,128)} %map_ref.7, s32[64,2048]{1,0:T(8,128)} %codes_ref.7, bf16[64,4096]{1,0:T(8,128)(2,1)} %weights_ref.3, f32[512,4,128]{2,1,0:T(4,128)} %bitcast.35), custom_call_target="tpu_custom_call" | custom-call | tf_op jit(solution)/shard_map/errors/pallas_call | solution.py:83
  16.1 1.3 copy.15
  17.4 19.2 %all_to_all.38 = f32[64,8,512]{2,0,1:T(8,128)} all-to-all(f32[64,8,512]{2,0,1:T(8,128)S(1)} %bitcast.39), channel_id=1, replica_groups=mesh['row'=4,'col'=8] {'col'}, dimensions={1} | all-to-all | bytes 2097152 | tf_op jit(solution)/shard_map/all_to_all | solution.py:335
  36.6 0.0 all-gather.3.cloned.1.call-update
  36.7 0.0 all-gather.5.cloned.1.call-start
  36.7 33.8 %split_hessian.1 = (bf16[4096,2048]{1,0:T(8,128)(2,1)}, bf16[4096,2048]{1,0:T(8,128)(2,1)}) custom-call(f32[65536,128]{1,0:T(8,128)} %bitcast.30), custom_call_target="tpu_custom_call" | custom-call | flops 33554432 | bytes 67108864 | tf_op jit(solution)/shard_map/split_hessian/pallas_call | solution.py:38
  70.5 46.9 %all-gather.3.cloned.1.call-done.error_ref = f32[512,2048]{1,0:T(8,128)} async-done(((f32[512,512]{1,0:T(8,128)}), f32[512,2048]{1,0:T(8,128)}) %all-gather.3.cloned.1.call-update) | async-done | bytes 4194320 | tf_op jit(solution)/shard_map/all_gather | solution.py:336
  117.3 60.0 %product.2.grad_ref = f32[64,4096]{1,0:T(8,128)} custom-call(f32[512,2048]{1,0:T(8,128)} %all-gather.3.cloned.1.call-done.error_ref, bf16[4096,2048]{1,0:T(8,128)(2,1)} %get-tuple-element.7.high_ref, bf16[4096,2048]{1,0:T(8,128)(2,1)} %get-tuple-element.8.low_ref), custom_call_target="tpu_custom_call" | custom-call | flops 25769803776 | bytes 46137344 | tf_op jit(solution)/shard_map/product/pallas_call | solution.py:175
  177.3 22.5 %scatter.2 = f32[512,4,128]{2,1,0:T(4,128)} custom-call(s32[4,16]{1,0:T(4,128)} %map_ref.7, s32[64,2048]{1,0:T(8,128)} %codes_ref.7, f32[64,4096]{1,0:T(8,128)} %product.2.grad_ref), custom_call_target="tpu_custom_call" | custom-call | tf_op jit(solution)/shard_map/scatter/pallas_call | solution.py:240
  199.8 38.8 %update.2.books_ref = f32[2048,128]{1,0:T(8,128)} custom-call(f32[2048,128]{1,0:T(8,128)} %bitcast.34, f32[2048,128]{1,0:T(8,128)} %bitcast.36), custom_call_target="tpu_custom_call" | custom-call | tf_op jit(solution)/shard_map/update/pallas_call | solution.py:306
  238.7 9.6 %errors.3 = f32[64,4096]{1,0:T(8,128)} custom-call(s32[4,16]{1,0:T(4,128)} %map_ref.7, s32[64,2048]{1,0:T(8,128)} %codes_ref.7, bf16[64,4096]{1,0:T(8,128)(2,1)} %weights_ref.3, f32[512,4,128]{2,1,0:T(4,128)} %bitcast.31), custom_call_target="tpu_custom_call" | custom-call | tf_op jit(solution)/shard_map/errors/pallas_call | solution.py:83
  248.2 1.3 copy.14
  249.5 16.9 %all_to_all.39 = f32[64,8,512]{2,0,1:T(8,128)} all-to-all(f32[64,8,512]{2,0,1:T(8,128)S(1)} %bitcast.40), channel_id=1, replica_groups=mesh['row'=4,'col'=8] {'col'}, dimensions={1} | all-to-all | bytes 2097152 | tf_op jit(solution)/shard_map/all_to_all | solution.py:335
  266.4 0.0 all-gather.5.cloned.1.call-update
  266.4 79.8 %all-gather.5.cloned.1.call-done.error_ref = f32[512,2048]{1,0:T(8,128)} async-done(((f32[512,512]{1,0:T(8,128)}), f32[512,2048]{1,0:T(8,128)}) %all-gather.5.cloned.1.call-update) | async-done | bytes 4194320 | tf_op jit(solution)/shard_map/all_gather | solution.py:336
  346.2 59.9 %product.3.grad_ref = f32[64,4096]{1,0:T(8,128)} custom-call(f32[512,2048]{1,0:T(8,128)} %all-gather.5.cloned.1.call-done.error_ref, bf16[4096,2048]{1,0:T(8,128)(2,1)} %get-tuple-element.7.high_ref, bf16[4096,2048]{1,0:T(8,128)(2,1)} %get-tuple-element.8.low_ref), custom_call_target="tpu_custom_call" | custom-call | flops 25769803776 | bytes 46137344 | tf_op jit(solution)/shard_map/product/pallas_call | solution.py:175
  406.1 22.5 %scatter.3 = f32[512,4,128]{2,1,0:T(4,128)} custom-call(s32[4,16]{1,0:T(4,128)} %map_ref.7, s32[64,2048]{1,0:T(8,128)} %codes_ref.7, f32[64,4096]{1,0:T(8,128)} %product.3.grad_ref), custom_call_target="tpu_custom_call" | custom-call | tf_op jit(solution)/shard_map/scatter/pallas_call | solution.py:240
  428.6 38.8 %update.3 = f32[2048,128]{1,0:T(8,128)} custom-call(f32[2048,128]{1,0:T(8,128)} %bitcast.32, f32[2048,128]{1,0:T(8,128)} %update.2.books_ref), custom_call_target="tpu_custom_call" | custom-call | tf_op jit(solution)/shard_map/update/pallas_call | solution.py:306
  467.5 2.6 copy.17
Async XLA Ops:
  6.5 110.8 %all-gather.3.cloned.1.call-start = ((), (), s32[]{:S(2)}) async-start(), calls=%async_computation.2 | async-start | bytes 5242880 | tf_op jit(solution)/shard_map/all_gather | solution.py:336
  36.7 309.5 %all-gather.5.cloned.1.call-start = ((), (), s32[]{:S(2)}) async-start(), calls=%async_computation.3 | async-start | bytes 5242880 | tf_op jit(solution)/shard_map/all_gather | solution.py:336
Sparse Core Ops, SparseCore 0:
  36.8 80.5 all-gather.2
  266.5 79.5 all-gather.4

commit v3 on v2

--- a/solution.py
+++ b/solution.py
@@ -50,29 +50,81 @@
     return jnp.take_along_axis(table, index, axis=1, mode="promise_in_bounds")
 
 
+def lookup(table, code):
+    index = code & (LANES - 1)
+    upper = code >= LANES
+    tables = [jnp.broadcast_to(table[n : n + 1, :], code.shape) for n in range(4)]
+    even = jnp.where(upper, pick(tables[2], index), pick(tables[0], index))
+    odd = jnp.where(upper, pick(tables[3], index), pick(tables[1], index))
+    return even, odd
+
+
 def error_kernel(map_ref, codes_ref, weights_ref, books_ref, error_ref):
     tiles_down, tiles_across = map_ref.shape
-    shape = (TILE_ROWS, LANES)
-    lane = lax.broadcasted_iota(jnp.int32, shape, 1)
-    odd = (lane & 1) == 1
+    lane = lax.broadcasted_iota(jnp.int32, (TILE_ROWS, LANES), 1)
+    is_odd = (lane & 1) == 1
 
     def tile(t, carry):
         i, j = t // tiles_across, t % tiles_across
-        table = books_ref[map_ref[i, j]]
         rows = pl.ds(pl.multiple_of(i * TILE_ROWS, TILE_ROWS), TILE_ROWS)
         codes = codes_ref[rows, pl.ds(pl.multiple_of(j * HALF, HALF), HALF)]
-        tables = [jnp.broadcast_to(table[n : n + 1, :], shape) for n in range(4)]
+        even, odd = lookup(books_ref[map_ref[i, j]], codes)
         for half in range(2):
-            code = pick(codes, (lane >> 1) + half * (LANES // 2))
-            index = code & (LANES - 1)
-            upper = code >= LANES
-            near = jnp.where(odd, pick(tables[1], index), pick(tables[0], index))
-            far = jnp.where(odd, pick(tables[3], index), pick(tables[2], index))
+            source = (lane >> 1) + half * (LANES // 2)
+            value = jnp.where(is_odd, pick(odd, source), pick(even, source))
             columns = pl.ds(pl.multiple_of(j * TILE_COLS + half * LANES, LANES), LANES)
-            error_ref[rows, columns] = jnp.where(upper, far, near) - weights_ref[rows, columns].astype(jnp.float32)
+            error_ref[rows, columns] = value - weights_ref[rows, columns].astype(jnp.float32)
         return carry
 
-    lax.fori_loop(0, tiles_down * tiles_across, tile, 0, unroll=2)
+    lax.fori_loop(0, tiles_down * tiles_across, tile, 0, unroll=4)
+
+
+def shift_kernel(run, gap, col_ref, map_ref, codes_ref, error_ref, new_ref, old_ref, out_ref):
+    rows_here, pairs = codes_ref.shape
+    down, across = rows_here // TILE_ROWS, pairs // HALF
+    top = pl.program_id(0) * down
+    lane = lax.broadcasted_iota(jnp.int32, (TILE_ROWS, LANES), 1)
+    is_odd = (lane & 1) == 1
+    begin = col_ref[0] * run
+
+    def table(i, column):
+        place = (column // run) * gap + begin + column % run
+        book = map_ref[top + i, place // TILE_COLS]
+        return new_ref[book] - old_ref[book]
+
+    def tile(t, carry):
+        i, j = t // across, t % across
+        rows = pl.ds(pl.multiple_of(i * TILE_ROWS, TILE_ROWS), TILE_ROWS)
+        codes = codes_ref[rows, pl.ds(pl.multiple_of(j * HALF, HALF), HALF)]
+        even, odd = lookup(table(i, j * TILE_COLS), codes)
+        if run % TILE_COLS:
+            even2, odd2 = lookup(table(i, j * TILE_COLS + LANES), codes)
+            second = lane >= LANES // 2
+            even, odd = jnp.where(second, even2, even), jnp.where(second, odd2, odd)
+        for half in range(2):
+            source = (lane >> 1) + half * (LANES // 2)
+            value = jnp.where(is_odd, pick(odd, source), pick(even, source))
+            columns = pl.ds(pl.multiple_of(j * TILE_COLS + half * LANES, LANES), LANES)
+            out_ref[rows, columns] = error_ref[rows, columns] + value
+        return carry
+
+    lax.fori_loop(0, down * across, tile, 0, unroll=4)
+
+
+def shift(run, gap, full_map, codes, error, new, old):
+    m, k = error.shape
+    block = min(m, 128)
+    col = jnp.full((1,), lax.axis_index("col"), jnp.int32)
+    books = pl.BlockSpec((new.shape[0] // 4, 4, LANES), lambda i: (0, 0, 0))
+    spec = pl.BlockSpec((block, k), lambda i: (i, 0))
+    return pl.pallas_call(
+        functools.partial(shift_kernel, run, gap),
+        grid=(m // block,),
+        in_specs=[SMEM, SMEM, pl.BlockSpec((block, k // 2), lambda i: (i, 0)), spec, books, books],
+        out_specs=spec,
+        out_shape=jax.ShapeDtypeStruct((m, k), jnp.float32),
+        name="shift",
+    )(col, full_map, codes, error, new.reshape(-1, 4, LANES), old.reshape(-1, 4, LANES))
 
 
 VMEM = pl.BlockSpec(memory_space=pltpu.VMEM)
@@ -233,7 +285,7 @@
         books_ref[book] += sums[0:4, :] + sums[4:8, :]
         return carry
 
-    lax.fori_loop(0, tiles_down * tiles_across, tile, 0)
+    lax.fori_loop(0, tiles_down * tiles_across, tile, 0, unroll=2)
 
 
 def scatter(tile_map, codes, grad, books):
@@ -330,12 +382,24 @@
     count, parts, entries = codebooks.shape
     books = codebooks.reshape(count, parts, entries // LANES, LANES).transpose(0, 2, 1, 3).reshape(-1, LANES)
     high, low = split_hessian(hessian)
+    run = hessian.shape[2] * hessian.shape[3]
+    maps = lax.all_gather(tile_map, ("row", "col"), axis=0)
+    full_map = maps.reshape(n_row, n_col, *tile_map.shape).transpose(1, 2, 0, 3)
+    full_map = full_map.reshape(n_col * tile_map.shape[0], n_row * tile_map.shape[1])
+    error = errors(tile_map, codes, weights, books)
+    piece = lax.all_to_all(error, "col", split_axis=1, concat_axis=0, tiled=True)
+    piece, full_map, held_codes = lax.optimization_barrier((piece, full_map, codes))
+    spread = lax.all_gather(piece, "row", axis=1, tiled=True)
+    code_piece = lax.all_to_all(held_codes, "col", split_axis=1, concat_axis=0, tiled=True)
+    code_spread = None
     for step in range(STEPS):
-        error = errors(tile_map, codes, weights, books)
-        piece = lax.all_to_all(error, "col", split_axis=1, concat_axis=0, tiled=True)
-        spread = lax.all_gather(piece, "row", axis=1, tiled=True)
         grad = product(n_col, spread, high, low)
-        books = update(n_row, n_col, scatter(tile_map, codes, grad, books), books)
+        if code_spread is None:
+            grad, code_piece = lax.optimization_barrier((grad, code_piece))
+            code_spread = lax.all_gather(code_piece, "row", axis=1, tiled=True)
+        old, books = books, update(n_row, n_col, scatter(tile_map, codes, grad, books), books)
+        if step < STEPS - 1:
+            spread = shift(run, n_col * run, full_map, code_spread, spread, books, old)
     return books.reshape(count, entries // LANES, parts, LANES).transpose(0, 2, 1, 3).reshape(codebooks.shape)
 
 

time: 478 us -> 416 us (0.87)
  waiting for transfers between devices: 127 us -> 38.1 us
  blocking collectives: 36.1 us -> 47.5 us
  starting transfers between devices: 0.04 us -> 8.89 us
    all_gather x2 -> x1, waiting for transfers between devices: 127 us -> 38 us  [per_device(): spread = lax.all_gather(piece, 'row', axis=1, tiled=True)]
    all_gather x0 -> x1, blocking collectives: none -> 47.5 us  [per_device(): maps = lax.all_gather(tile_map, ('row', 'col'), axis=0)]
    all_to_all x2 -> x0, blocking collectives: 36.1 us -> none  [per_device(): lax.all_to_all(error, 'col', split_axis=1, concat_axis=0, tiled=True)]
    pallas_call x0 -> x1, Pallas kernels: none -> 18.7 us  [shift(): pl.pallas_call(functools.partial(shift_kernel, run, gap), grid=(m // bloc...]
    pallas_call x2 -> x1, Pallas kernels: 19.1 us -> 6.09 us  [errors(): pl.pallas_call(error_kernel, in_specs=[SMEM, VMEM, VMEM, VMEM], out_specs...]
    pallas_call x2, Pallas kernels: 45 us -> 34.2 us  [scatter(): pl.pallas_call(scatter_kernel, in_specs=[SMEM, VMEM, VMEM], out_specs=VME...]
    all_to_all x0 -> x2, starting transfers between devices: none -> 8.78 us  [the longest x1 5.21 us: per_device(): lax.all_to_all(error, 'col', split_axis=1, concat_axis=0, tiled=True)]
    pallas_call x2, Pallas kernels: 77.7 us -> 85.9 us  [update(): pl.pallas_call(functools.partial(update_kernel, n_row, n_col), in_specs=[...]
  transfers between devices with their start and end apart: 2 -> 4, of which waited for: 2 -> 1; matrix products, arithmetic and copies ran while one was open for 0% -> 0% of each run, Pallas kernels for 7% -> 37%
where the time goes in v3:
time: 416 us; the launch traced here: 415 us
  Pallas kernels  299 us (72%)
  blocking collectives  47.5 us (11%)
  waiting for transfers between devices  38.1 us (9%)
  between operations  13.5 us (3%)
  starting transfers between devices  8.89 us (2%)
  local copies, waits for them, and re-layouts  8.16 us (2%)
    pallas_call x2, Pallas kernels, product(): pl.pallas_call(functools.partial(product_kernel, chunks), grid=(chunks,),...  120 us
    pallas_call x2, Pallas kernels, update(): pl.pallas_call(functools.partial(update_kernel, n_row, n_col), in_specs=[...  85.9 us
    all_gather x1, blocking collectives, per_device(): maps = lax.all_gather(tile_map, ('row', 'col'), axis=0)  47.5 us
    all_gather x1, waiting for transfers between devices, per_device(): spread = lax.all_gather(piece, 'row', axis=1, tiled=True)  38 us
    pallas_call x2, Pallas kernels, scatter(): pl.pallas_call(scatter_kernel, in_specs=[SMEM, VMEM, VMEM], out_specs=VME...  34.2 us
    pallas_call x1, Pallas kernels, split_hessian(): pl.pallas_call(split_kernel, grid=(rows // block,), in_specs=[pl.BlockSpe...  33.8 us
    pallas_call x1, Pallas kernels, shift(): pl.pallas_call(functools.partial(shift_kernel, run, gap), grid=(m // bloc...  18.7 us
  transfers between devices with their start and end apart: 4, of which 1 were waited for; matrix products, arithmetic and copies ran while one was open for 0% of the time, Pallas kernels for 37%

profile of v3, /device:TPU:1, one launch (start us, length us, event | category | flops | bytes accessed | tf_op | source)
XLA Modules:
  0.0 414.8 jit_solution(7704063916686590516)
XLA Ops:
  6.5 6.1 %errors.1 = f32[64,4096]{1,0:T(8,128)} custom-call(s32[4,16]{1,0:T(4,128)} %map_ref.5, s32[64,2048]{1,0:T(8,128)} %codes_ref.5, bf16[64,4096]{1,0:T(8,128)(2,1)} %weights_ref.1, f32[512,4,128]{2,1,0:T(4,128)} %bitcast.38), custom_call_target="tpu_custom_call" | custom-call | tf_op jit(solution)/shard_map/errors/pallas_call | solution.py:135
  12.6 2.3 copy.21
  14.9 5.2 %all-to-all-start = ((f32[64,8,512]{2,0,1:T(8,128)}), f32[64,8,512]{2,0,1:T(8,128)S(1)}, u32[]{:S(2)}, u32[]{:S(2)}) async-start(f32[64,8,512]{2,0,1:T(8,128)} %bitcast.33), calls=%async_computation | async-start | bytes 2097152 | tf_op jit(solution)/shard_map/all_to_all | solution.py:390
  20.1 0.0 all-gather.5.cloned.1.call-start
  20.1 47.5 %all-gather.1 = s32[32,4,16]{2,1,0:T(4,128)S(1)} all-gather(s32[1,4,16]{2,1,0:T(4,128)} %bitcast.50), channel_id=2, replica_groups=mesh['row'=4,'col'=8] {'row','col'}, dimensions={0}, use_global_device_ids=true | all-gather | bytes 8448 | tf_op jit(solution)/shard_map/all_gather | solution.py:386
  67.7 0.7 reshape.38.map_ref
  68.4 0.0 all-to-all-done
  68.4 0.0 copy-start.1
  68.4 1.0 copy-done.1
  69.4 0.0 all-gather.5.cloned.1.call-update
  69.4 0.0 copy-start
  69.4 33.8 %split_hessian.1 = (bf16[4096,2048]{1,0:T(8,128)(2,1)}, bf16[4096,2048]{1,0:T(8,128)(2,1)}) custom-call(f32[65536,128]{1,0:T(8,128)} %bitcast.36), custom_call_target="tpu_custom_call" | custom-call | flops 33554432 | bytes 67108864 | tf_op jit(solution)/shard_map/split_hessian/pallas_call | solution.py:38
  103.2 0.0 copy-done
  103.2 0.8 copy.22
  104.1 3.6 all-to-all-start.1
  107.6 0.1 all-gather.7.cloned.1.call-start
  107.7 38.0 %all-gather.5.cloned.1.call-done.error_ref = f32[512,2048]{1,0:T(8,128)} async-done(((f32[512,512]{1,0:T(8,128)}), f32[512,2048]{1,0:T(8,128)}) %all-gather.5.cloned.1.call-update) | async-done | bytes 4194320 | tf_op jit(solution)/shard_map/all_gather | solution.py:392
  145.8 60.0 %product.2.grad_ref = f32[64,4096]{1,0:T(8,128)} custom-call(f32[512,2048]{1,0:T(8,128)} %all-gather.5.cloned.1.call-done.error_ref, bf16[4096,2048]{1,0:T(8,128)(2,1)} %get-tuple-element.14.high_ref, bf16[4096,2048]{1,0:T(8,128)(2,1)} %get-tuple-element.15.low_ref), custom_call_target="tpu_custom_call" | custom-call | flops 25769803776 | bytes 46137344 | tf_op jit(solution)/shard_map/product/pallas_call | solution.py:227
  205.7 0.0 all-to-all-done.1
  205.8 0.0 copy-start.2
  205.8 0.8 copy-done.2
  206.5 0.0 all-gather.7.cloned.1.call-update
  206.6 17.1 %scatter.2 = f32[512,4,128]{2,1,0:T(4,128)} custom-call(s32[4,16]{1,0:T(4,128)} %map_ref.5, s32[64,2048]{1,0:T(8,128)} %codes_ref.5, f32[64,4096]{1,0:T(8,128)} %product.2.grad_ref), custom_call_target="tpu_custom_call" | custom-call | tf_op jit(solution)/shard_map/scatter/pallas_call | solution.py:292
  223.7 43.8 %update.2.books_ref = f32[2048,128]{1,0:T(8,128)} custom-call(f32[2048,128]{1,0:T(8,128)} %bitcast.44, f32[2048,128]{1,0:T(8,128)} %bitcast.39), custom_call_target="tpu_custom_call" | custom-call | tf_op jit(solution)/shard_map/update/pallas_call | solution.py:358
  267.5 0.0 all-gather.7.cloned.1.call-done.codes_ref
  267.5 18.7 %shift.1.error_ref = f32[512,2048]{1,0:T(8,128)} custom-call(s32[1]{0:T(128)} %bitcast.col_ref, s32[32,64]{1,0:T(8,128)} %reshape.38.map_ref, s32[512,1024]{1,0:T(8,128)} %all-gather.7.cloned.1.call-done.codes_ref, f32[512,2048]{1,0:T(8,128)} %all-gather.5.cloned.1.call-done.error_ref, f32[512,4,128]{2,1,0:T(4,128)} %bitcast.37, f32[512,4,128]{2,1,0:T(4,128)} %bitcast.40), custom_call_target="tpu_custom_call" | custom-call | tf_op jit(solution)/shard_map/shift/pallas_call | solution.py:120
  286.2 59.9 %product.3.grad_ref = f32[64,4096]{1,0:T(8,128)} custom-call(f32[512,2048]{1,0:T(8,128)} %shift.1.error_ref, bf16[4096,2048]{1,0:T(8,128)(2,1)} %get-tuple-element.14.high_ref, bf16[4096,2048]{1,0:T(8,128)(2,1)} %get-tuple-element.15.low_ref), custom_call_target="tpu_custom_call" | custom-call | flops 25769803776 | bytes 46137344 | tf_op jit(solution)/shard_map/product/pallas_call | solution.py:227
  346.1 17.1 %scatter.3 = f32[512,4,128]{2,1,0:T(4,128)} custom-call(s32[4,16]{1,0:T(4,128)} %map_ref.5, s32[64,2048]{1,0:T(8,128)} %codes_ref.5, f32[64,4096]{1,0:T(8,128)} %product.3.grad_ref), custom_call_target="tpu_custom_call" | custom-call | tf_op jit(solution)/shard_map/scatter/pallas_call | solution.py:292
  363.2 42.2 %update.3 = f32[2048,128]{1,0:T(8,128)} custom-call(f32[2048,128]{1,0:T(8,128)} %bitcast.42, f32[2048,128]{1,0:T(8,128)} %update.2.books_ref), custom_call_target="tpu_custom_call" | custom-call | tf_op jit(solution)/shard_map/update/pallas_call | solution.py:358
  405.4 2.6 copy.25
  (1 shorter events, 0.0 us)
Async XLA Ops:
  14.9 53.5 %all-to-all-start = ((f32[64,8,512]{2,0,1:T(8,128)}), f32[64,8,512]{2,0,1:T(8,128)S(1)}, u32[]{:S(2)}, u32[]{:S(2)}) async-start(f32[64,8,512]{2,0,1:T(8,128)} %bitcast.33), calls=%async_computation | async-start | bytes 2097152 | tf_op jit(solution)/shard_map/all_to_all | solution.py:390
  20.1 125.6 %all-gather.5.cloned.1.call-start = ((), (), s32[]{:S(2)}) async-start(), calls=%async_computation.2 | async-start | bytes 5242880 | tf_op jit(solution)/shard_map/all_gather | solution.py:392
  68.4 1.0 copy-start.1
  69.4 33.8 %copy-start = (s32[64,2048]{1,0:T(8,128)S(1)}, s32[64,2048]{1,0:T(8,128)}, u32[]{:S(2)}) copy-start(s32[64,2048]{1,0:T(8,128)} %codes_ref.5) | copy-start | bytes 1572868
  104.1 101.7 %all-to-all-start.1 = ((s32[64,8,256]{2,0,1:T(8,128)}), s32[64,8,256]{2,0,1:T(8,128)S(1)}, u32[]{:S(2)}, u32[]{:S(2)}) async-start(s32[64,8,256]{2,0,1:T(8,128)} %bitcast.34), calls=%async_computation.1 | async-start | bytes 1048576 | tf_op jit(solution)/shard_map/all_to_all | solution.py:393
  107.6 159.8 %all-gather.7.cloned.1.call-start = ((), (), s32[]{:S(2)}) async-start(), calls=%async_computation.3 | async-start | bytes 2621440 | tf_op jit(solution)/shard_map/all_gather | solution.py:399
  205.8 0.8 copy-start.2
Sparse Core Ops, SparseCore 0:
  69.5 76.1 all-gather.4
  206.7 50.2 all-gather.6

commit v4 on v3

--- a/solution.py
+++ b/solution.py
@@ -299,7 +299,7 @@
     return total.reshape(books.shape)
 
 
-def update_kernel(n_row, n_col, grad_ref, books_ref, out_ref, col_in, row_sum, row_in, col_send, col_recv, row_send, row_recv, row_send2, row_recv2, col_send2, col_recv2):
+def update_kernel(n_row, n_col, grad_ref, books_ref, map_ref, out_ref, maps_ref, col_in, row_sum, row_in, col_send, col_recv, row_send, row_recv, row_send2, row_recv2, col_send2, col_recv2, map_send, map_recv, map_send2, map_recv2):
     r, c = lax.axis_index("row"), lax.axis_index("col")
     wide = grad_ref.shape[0] // n_col
     thin = wide // n_row
@@ -326,6 +326,8 @@
     first = [
         send(grad_ref.at[piece(cols[d], wide)], col_in.at[d], col_send, col_recv, d, (r, cols[d])) for d in range(1, n_col)
     ]
+    maps = [send(map_ref, maps_ref.at[r, c], map_send, map_recv, d, (r, cols[d])) for d in range(1, n_col)]
+    maps_ref[r, c] = map_ref[...]
     total = grad_ref[piece(c, wide), :]
     for d, copy in enumerate(first, 1):
         copy.wait_recv()
@@ -334,6 +336,9 @@
     second = [
         send(row_sum.at[piece(rows[d], thin)], row_in.at[d], row_send, row_recv, d, (rows[d], c)) for d in range(1, n_row)
     ]
+    for copy in maps:
+        copy.wait_recv()
+    lines = [send(maps_ref.at[r], maps_ref.at[r], map_send2, map_recv2, d, (rows[d], c)) for d in range(1, n_row)]
     total = row_sum[piece(r, thin), :]
     for d, copy in enumerate(second, 1):
         copy.wait_recv()
@@ -347,19 +352,24 @@
     fourth = [send(out_ref.at[whole], out_ref.at[whole], col_send2, col_recv2, d, (r, cols[d])) for d in range(1, n_col)]
     for copy in fourth:
         copy.wait_recv()
-    for copy in first + second + third + fourth:
+    for copy in lines:
+        copy.wait_recv()
+    for copy in first + second + third + fourth + maps + lines:
         copy.wait_send()
 
 
-def update(n_row, n_col, grad, books):
+def update(n_row, n_col, grad, books, padded):
     wide = books.shape[0] // n_col
     thin = wide // n_row
     dma = pltpu.SemaphoreType.DMA
     return pl.pallas_call(
         functools.partial(update_kernel, n_row, n_col),
-        in_specs=[VMEM, VMEM],
-        out_specs=VMEM,
-        out_shape=jax.ShapeDtypeStruct(books.shape, jnp.float32),
+        in_specs=[VMEM, VMEM, VMEM],
+        out_specs=[VMEM, VMEM],
+        out_shape=[
+            jax.ShapeDtypeStruct(books.shape, jnp.float32),
+            jax.ShapeDtypeStruct((n_row, n_col) + padded.shape, jnp.int32),
+        ],
         scratch_shapes=[
             pltpu.VMEM((n_col, wide, LANES), jnp.float32),
             pltpu.VMEM((wide, LANES), jnp.float32),
@@ -372,10 +382,14 @@
             dma((n_row,)),
             dma((n_col,)),
             dma((n_col,)),
+            dma((n_col,)),
+            dma((n_col,)),
+            dma((n_row,)),
+            dma((n_row,)),
         ],
         compiler_params=pltpu.CompilerParams(collective_id=0, has_side_effects=True),
         name="update",
-    )(grad, books)
+    )(grad, books, padded)
 
 
 def per_device(n_row, n_col, hessian, weights, codes, tile_map, codebooks):
@@ -383,12 +397,11 @@
     books = codebooks.reshape(count, parts, entries // LANES, LANES).transpose(0, 2, 1, 3).reshape(-1, LANES)
     high, low = split_hessian(hessian)
     run = hessian.shape[2] * hessian.shape[3]
-    maps = lax.all_gather(tile_map, ("row", "col"), axis=0)
-    full_map = maps.reshape(n_row, n_col, *tile_map.shape).transpose(1, 2, 0, 3)
-    full_map = full_map.reshape(n_col * tile_map.shape[0], n_row * tile_map.shape[1])
+    down, across = tile_map.shape
+    padded = jnp.pad(tile_map, ((0, -down % 8), (0, -across % LANES)))
     error = errors(tile_map, codes, weights, books)
     piece = lax.all_to_all(error, "col", split_axis=1, concat_axis=0, tiled=True)
-    piece, full_map, held_codes = lax.optimization_barrier((piece, full_map, codes))
+    piece, held_codes = lax.optimization_barrier((piece, codes))
     spread = lax.all_gather(piece, "row", axis=1, tiled=True)
     code_piece = lax.all_to_all(held_codes, "col", split_axis=1, concat_axis=0, tiled=True)
     code_spread = None
@@ -397,8 +410,10 @@
         if code_spread is None:
             grad, code_piece = lax.optimization_barrier((grad, code_piece))
             code_spread = lax.all_gather(code_piece, "row", axis=1, tiled=True)
-        old, books = books, update(n_row, n_col, scatter(tile_map, codes, grad, books), books)
+        old = books
+        books, maps = update(n_row, n_col, scatter(tile_map, codes, grad, books), books, padded)
         if step < STEPS - 1:
+            full_map = maps[:, :, :down, :across].transpose(1, 2, 0, 3).reshape(n_col * down, n_row * across)
             spread = shift(run, n_col * run, full_map, code_spread, spread, books, old)
     return books.reshape(count, entries // LANES, parts, LANES).transpose(0, 2, 1, 3).reshape(codebooks.shape)
 

time: 416 us -> 390 us (0.938)
  blocking collectives: 47.5 us -> 19.2 us
  starting transfers between devices: 8.89 us -> 4.59 us
    all_gather x1 -> x0, blocking collectives: 47.5 us -> none  [per_device(): maps = lax.all_gather(tile_map, ('row', 'col'), axis=0)]
    all_to_all x0 -> x1, blocking collectives: none -> 19.2 us  [per_device(): lax.all_to_all(error, 'col', split_axis=1, concat_axis=0, tiled=True)]
    all_to_all x1 -> x0, starting transfers between devices: 5.21 us -> none  [per_device(): lax.all_to_all(error, 'col', split_axis=1, concat_axis=0, tiled=True)]
  transfers between devices with their start and end apart: 4 -> 3, of which waited for: 1 -> 1; matrix products, arithmetic and copies ran while one was open for 0% -> 1% of each run, Pallas kernels for 37% -> 41%
where the time goes in v4:
time: 390 us; the launch traced here: 389 us
  Pallas kernels  302 us (77%)
  waiting for transfers between devices  41.5 us (11%)
  blocking collectives  19.2 us (5%)
  between operations  13.5 us (3%)
  local copies, waits for them, and re-layouts  7.75 us (2%)
  starting transfers between devices  4.59 us (1%)
    pallas_call x2, Pallas kernels, product(): pl.pallas_call(functools.partial(product_kernel, chunks), grid=(chunks,),...  120 us
    pallas_call x2, Pallas kernels, update(): pl.pallas_call(functools.partial(update_kernel, n_row, n_col), in_specs=[...  89.6 us
    all_gather x1, waiting for transfers between devices, per_device(): spread = lax.all_gather(piece, 'row', axis=1, tiled=True)  41.4 us
    pallas_call x2, Pallas kernels, scatter(): pl.pallas_call(scatter_kernel, in_specs=[SMEM, VMEM, VMEM], out_specs=VME...  34.2 us
    pallas_call x1, Pallas kernels, split_hessian(): pl.pallas_call(split_kernel, grid=(rows // block,), in_specs=[pl.BlockSpe...  33.8 us
    all_to_all x1, blocking collectives, per_device(): lax.all_to_all(error, 'col', split_axis=1, concat_axis=0, tiled=True)  19.2 us
    pallas_call x1, Pallas kernels, shift(): pl.pallas_call(functools.partial(shift_kernel, run, gap), grid=(m // bloc...  18.6 us
  transfers between devices with their start and end apart: 3, of which 1 were waited for; matrix products, arithmetic and copies ran while one was open for 1% of the time, Pallas kernels for 41%

profile of v4, /device:TPU:1, one launch (start us, length us, event | category | flops | bytes accessed | tf_op | source)
XLA Modules:
  0.0 388.9 jit_solution(237079612428604356)
XLA Ops:
  6.5 0.0 all-gather.3.cloned.1.call-start
  6.5 6.1 %errors.1 = f32[64,4096]{1,0:T(8,128)} custom-call(s32[4,16]{1,0:T(4,128)} %map_ref.5, s32[64,2048]{1,0:T(8,128)} %codes_ref.5, bf16[64,4096]{1,0:T(8,128)(2,1)} %weights_ref.1, f32[512,4,128]{2,1,0:T(4,128)} %bitcast.34), custom_call_target="tpu_custom_call" | custom-call | tf_op jit(solution)/shard_map/errors/pallas_call | solution.py:135
  12.6 1.3 copy.15
  13.9 19.2 %all_to_all.38 = f32[64,8,512]{2,0,1:T(8,128)} all-to-all(f32[64,8,512]{2,0,1:T(8,128)S(1)} %bitcast.42), channel_id=1, replica_groups=mesh['row'=4,'col'=8] {'col'}, dimensions={1} | all-to-all | bytes 2097152 | tf_op jit(solution)/shard_map/all_to_all | solution.py:403
  33.2 0.0 all-gather.3.cloned.1.call-update
  33.2 0.0 copy-start
  33.2 33.8 %split_hessian.1 = (bf16[4096,2048]{1,0:T(8,128)(2,1)}, bf16[4096,2048]{1,0:T(8,128)(2,1)}) custom-call(f32[65536,128]{1,0:T(8,128)} %bitcast.33), custom_call_target="tpu_custom_call" | custom-call | flops 33554432 | bytes 67108864 | tf_op jit(solution)/shard_map/split_hessian/pallas_call | solution.py:38
  67.0 0.0 copy-done
  67.0 0.8 copy.16
  67.8 4.6 %all-to-all-start.1 = ((s32[64,8,256]{2,0,1:T(8,128)}), s32[64,8,256]{2,0,1:T(8,128)S(1)}, u32[]{:S(2)}, u32[]{:S(2)}) async-start(s32[64,8,256]{2,0,1:T(8,128)} %bitcast.32), calls=%async_computation.1 | async-start | bytes 1048576 | tf_op jit(solution)/shard_map/all_to_all | solution.py:406
  72.4 0.0 all-gather.5.cloned.1.call-start
  72.4 41.4 %all-gather.3.cloned.1.call-done.error_ref = f32[512,2048]{1,0:T(8,128)} async-done(((f32[512,512]{1,0:T(8,128)}), f32[512,2048]{1,0:T(8,128)}) %all-gather.3.cloned.1.call-update) | async-done | bytes 4194320 | tf_op jit(solution)/shard_map/all_gather | solution.py:405
  113.9 0.0 copy-start.2
  113.9 60.0 %product.2.grad_ref = f32[64,4096]{1,0:T(8,128)} custom-call(f32[512,2048]{1,0:T(8,128)} %all-gather.3.cloned.1.call-done.error_ref, bf16[4096,2048]{1,0:T(8,128)(2,1)} %get-tuple-element.15.high_ref, bf16[4096,2048]{1,0:T(8,128)(2,1)} %get-tuple-element.16.low_ref), custom_call_target="tpu_custom_call" | custom-call | flops 25769803776 | bytes 46137344 | tf_op jit(solution)/shard_map/product/pallas_call | solution.py:227
  173.8 0.0 all-to-all-done.1
  173.8 0.0 copy-start.1
  173.9 0.8 copy-done.1
  174.6 0.0 all-gather.5.cloned.1.call-update
  174.7 0.0 copy-done.2
  174.7 0.6 pad.4.map_ref
  175.3 17.1 %scatter.2 = f32[512,4,128]{2,1,0:T(4,128)} custom-call(s32[4,16]{1,0:T(4,128)} %map_ref.5, s32[64,2048]{1,0:T(8,128)} %codes_ref.5, f32[64,4096]{1,0:T(8,128)} %product.2.grad_ref), custom_call_target="tpu_custom_call" | custom-call | tf_op jit(solution)/shard_map/scatter/pallas_call | solution.py:292
  192.4 49.2 %update.2 = (f32[2048,128]{1,0:T(8,128)}, s32[4,8,8,128]{3,2,1,0:T(8,128)}) custom-call(f32[2048,128]{1,0:T(8,128)} %bitcast.41, f32[2048,128]{1,0:T(8,128)} %bitcast.35, s32[8,128]{1,0:T(8,128)} %pad.4.map_ref), custom_call_target="tpu_custom_call" | custom-call | tf_op jit(solution)/shard_map/update/pallas_call | solution.py:365
  241.6 0.9 slice_bitcast_fusion
  242.5 0.7 reshape.37.map_ref
  243.2 0.0 all-gather.5.cloned.1.call-done.codes_ref
  243.2 18.6 %shift.1.error_ref = f32[512,2048]{1,0:T(8,128)} custom-call(s32[1]{0:T(128)} %bitcast.col_ref, s32[32,64]{1,0:T(8,128)} %reshape.37.map_ref, s32[512,1024]{1,0:T(8,128)} %all-gather.5.cloned.1.call-done.codes_ref, f32[512,2048]{1,0:T(8,128)} %all-gather.3.cloned.1.call-done.error_ref, f32[512,4,128]{2,1,0:T(4,128)} %bitcast.38, f32[512,4,128]{2,1,0:T(4,128)} %bitcast.36), custom_call_target="tpu_custom_call" | custom-call | tf_op jit(solution)/shard_map/shift/pallas_call | solution.py:120
  261.9 60.1 %product.3.grad_ref = f32[64,4096]{1,0:T(8,128)} custom-call(f32[512,2048]{1,0:T(8,128)} %shift.1.error_ref, bf16[4096,2048]{1,0:T(8,128)(2,1)} %get-tuple-element.15.high_ref, bf16[4096,2048]{1,0:T(8,128)(2,1)} %get-tuple-element.16.low_ref), custom_call_target="tpu_custom_call" | custom-call | flops 25769803776 | bytes 46137344 | tf_op jit(solution)/shard_map/product/pallas_call | solution.py:227
  322.0 17.1 %scatter.3 = f32[512,4,128]{2,1,0:T(4,128)} custom-call(s32[4,16]{1,0:T(4,128)} %map_ref.5, s32[64,2048]{1,0:T(8,128)} %codes_ref.5, f32[64,4096]{1,0:T(8,128)} %product.3.grad_ref), custom_call_target="tpu_custom_call" | custom-call | tf_op jit(solution)/shard_map/scatter/pallas_call | solution.py:292
  339.1 40.4 %update.3 = (f32[2048,128]{1,0:T(8,128)}, s32[4,8,8,128]{3,2,1,0:T(8,128)}) custom-call(f32[2048,128]{1,0:T(8,128)} %bitcast.40, f32[2048,128]{1,0:T(8,128)} %get-tuple-element.21.books_ref, s32[8,128]{1,0:T(8,128)} %pad.4.map_ref), custom_call_target="tpu_custom_call" | custom-call | tf_op jit(solution)/shard_map/update/pallas_call | solution.py:365
  379.5 2.6 copy.18
  (1 shorter events, 0.0 us)
Async XLA Ops:
  6.5 107.3 %all-gather.3.cloned.1.call-start = ((), (), s32[]{:S(2)}) async-start(), calls=%async_computation.2 | async-start | bytes 5242880 | tf_op jit(solution)/shard_map/all_gather | solution.py:405
  33.2 33.8 %copy-start = (s32[64,2048]{1,0:T(8,128)S(1)}, s32[64,2048]{1,0:T(8,128)}, u32[]{:S(2)}) copy-start(s32[64,2048]{1,0:T(8,128)} %codes_ref.5) | copy-start | bytes 1572868
  67.8 106.0 %all-to-all-start.1 = ((s32[64,8,256]{2,0,1:T(8,128)}), s32[64,8,256]{2,0,1:T(8,128)S(1)}, u32[]{:S(2)}, u32[]{:S(2)}) async-start(s32[64,8,256]{2,0,1:T(8,128)} %bitcast.32), calls=%async_computation.1 | async-start | bytes 1048576 | tf_op jit(solution)/shard_map/all_to_all | solution.py:406
  72.4 170.8 %all-gather.5.cloned.1.call-start = ((), (), s32[]{:S(2)}) async-start(), calls=%async_computation.3 | async-start | bytes 2621440 | tf_op jit(solution)/shard_map/all_gather | solution.py:412
  113.9 60.8 %copy-start.2 = (s32[4,16]{1,0:T(4,128)S(1)}, s32[4,16]{1,0:T(4,128)}, u32[]{:S(2)}) copy-start(s32[4,16]{1,0:T(4,128)} %map_ref.5) | copy-start | bytes 772
  173.8 0.8 copy-start.1
Sparse Core Ops, SparseCore 0:
  33.3 80.5 all-gather.2
  174.8 52.8 all-gather.4
